TPU v7x, 32 devices: a whole 2x2x4 slice. The times are simulated.
32 devices in a mesh: groups: 2 (over x), ctx: 16 (over z, y, core).
Axes of the slice: x: 2, y: 2, z: 4, core: 2. Of those that a mesh axis runs over, the one named last changes fastest.
Arguments:
- queries: bfloat16 [256, 16, 128], P(('groups', 'ctx')), parts along dimension 0
- new_keys: bfloat16 [256, 128], P(('groups', 'ctx')), parts along dimension 0
- new_values: bfloat16 [256, 128], P(('groups', 'ctx')), parts along dimension 0, may hold values from -6 to 6
- pool_keys: bfloat16 [384, 128, 128], P(('groups', 'ctx')), parts along dimension 0, may hold values from -6 to 6
- pool_values: bfloat16 [384, 128, 128], P(('groups', 'ctx')), parts along dimension 0, may hold values from -6 to 6
- block_owner: int32 [32, 12], P('groups'), parts along dimension 0, may hold values from 0 to 15, as said below
- block_id: int32 [32, 12], P('groups'), parts along dimension 0, may hold values from 0 to 11
- old_start: int32 [32, 12], P('groups'), parts along dimension 0, may hold values from 0 to 24575
- cached_counts: int32 [32], P('groups'), parts along dimension 0, may hold values from 1 to 12, 168 in all
Outputs:
- attended: bfloat16 [256, 16, 128], P(('groups', 'ctx')), parts along dimension 0
There are 2 independent parts, one for each index of `groups`. A program takes and returns all parts, laid end to end along the dimension named above; each array names one. Nothing has to cross between parts.
Inputs may be any that keep to these rules, and one draw needn't show every extreme that they name: `block_owner`: row e lists the owners e, e + 1, ..., e + 12 - 1 modulo 16, each once, in a drawn order. `cached_counts`: entries sum to 168; entry e counts the slots of row e in use, always the first ones.
All inputs are finite; a program needn't handle non-finite values.
Results may differ from a plain program's by a relative error of at most 0.0109.
Values may be sent and summed in bfloat16 or wider, within the bound.
A program may use at most 64 MiB of HBM per device.

v0:
```python
import functools
import math

import jax
import jax.numpy as jnp
import numpy as np
from jax import lax
from jax.experimental import pallas as pl
from jax.experimental.pallas import tpu as pltpu
from jax.sharding import PartitionSpec as P

MESH = pl.DeviceIdType.MESH
NEG = -1e30
F32 = jnp.float32
BF16 = jnp.bfloat16


def frequencies(head):
    pair_index = np.arange(head // 2, dtype=np.float64)
    inverse = np.exp(-(2.0 * pair_index / head) * math.log(500000.0))
    wavelen = 2.0 * math.pi / inverse
    smooth = (8192.0 / wavelen - 1.0) / 3.0
    blended = (1.0 - smooth) * inverse / 8.0 + smooth * inverse
    freq = np.where(wavelen > 8192.0, inverse / 8.0, np.where(wavelen < 2048.0, inverse, blended))
    return np.tile(freq.astype(np.float32), (8, 2))


def pack(out, lse):
    cols = out.shape[1]
    hi = lse.astype(BF16).astype(F32)
    mid = (lse - hi).astype(BF16).astype(F32)
    low = lse - hi - mid
    row = lax.broadcasted_iota(jnp.int32, (16, cols), 0)
    tail = jnp.where(row == 0, hi, jnp.where(row == 1, mid, jnp.where(row == 2, low, 0.0)))
    return jnp.concatenate([out.astype(BF16), tail.astype(BF16)], axis=0)


def unpack(message, head):
    tail = message[head : head + 16].astype(F32)
    lse = tail[0:1] + tail[1:2] + tail[2:3]
    return message[:head].astype(F32), lse


def kernel(
    dims,
    q_ref,
    nk_ref,
    nv_ref,
    pk_ref,
    pv_ref,
    freq_ref,
    owner_ref,
    id_ref,
    old_ref,
    count_ref,
    o_ref,
    qbuf,
    pk_own,
    pv_own,
    pk_other,
    pv_other,
    nkbuf,
    nvbuf,
    kbuf,
    vbuf,
    sbuf,
    sbuf2,
    tbuf,
    tbuf2,
    wbuf,
    wbuf2,
    pbuf,
    outbuf,
    fbuf,
    prefix,
    l_sem,
    q_recv,
    z_send,
    y_send,
    x_send,
    x_recv,
    f_send,
    f_recv,
):
    n, nb, blk, head, rows, fresh, group = dims
    ny = 2
    nz = n // (2 * ny)
    chips = n // 2
    me = lax.axis_index("ctx")
    grp = lax.axis_index("groups")
    c = lax.rem(me, 2)
    chip = me // 2
    y = lax.rem(chip, ny)
    z = chip // ny
    other = me + 1 - 2 * c

    def z_at(k):
        if nz & (nz - 1):
            return lax.rem(z + k, nz)
        total, bit = 0, 1
        while bit < nz:
            total = total + lax.rem(z // bit + k // bit, 2) * bit
            bit *= 2
        return total

    def chip_at(k, b):
        return z_at(k) * ny + lax.rem(y + b, ny)

    barrier = pltpu.get_barrier_semaphore()
    for r in range(1, chips):
        pl.semaphore_signal(
            barrier, inc=1,
            device_id=(grp, 2 * lax.rem(chip + r, chips) + c), device_id_type=MESH,
        )
    pl.semaphore_signal(barrier, inc=1, device_id=(grp, other), device_id_type=MESH)

    load_q = pltpu.make_async_copy(q_ref, qbuf.at[chip], l_sem.at[0])
    load_k = pltpu.make_async_copy(pk_ref, pk_own, l_sem.at[1])
    load_v = pltpu.make_async_copy(pv_ref, pv_own, l_sem.at[2])
    load_q.start()
    load_k.start()
    load_v.start()
    load_q.wait()
    pl.semaphore_wait(barrier, chips)

    def copy(src, dst, ss, rs, to):
        return pltpu.make_async_remote_copy(
            src_ref=src, dst_ref=dst, send_sem=ss, recv_sem=rs,
            device_id=(grp, to), device_id_type=MESH,
        )

    def q_copy(slot, ss, to_chip):
        return copy(qbuf.at[slot], qbuf.at[slot], ss, q_recv.at[slot], 2 * to_chip + c)

    y_chip = chip_at(0, 1)
    far_first = [*range(2, nz), 1][: nz - 1]
    z_copies = [q_copy(chip, z_send.at[k], chip_at(k, 0)) for k in far_first]
    for d in z_copies:
        d.start()
    q_copy(chip, y_send.at[0], y_chip).start()
    shared = [
        copy(nk_ref, nkbuf, x_send.at[0], x_recv.at[0], other),
        copy(nv_ref, nvbuf, x_send.at[1], x_recv.at[1], other),
        copy(pk_ref, pk_other, x_send.at[2], x_recv.at[2], other),
        copy(pv_ref, pv_other, x_send.at[3], x_recv.at[3], other),
    ]
    for d in shared:
        d.start()

    total = jnp.int32(0)
    for e in range(n):
        prefix[e] = total
        total = total + count_ref[e]

    pad = -(-nb // 8) * 8
    row = lax.broadcasted_iota(jnp.int32, (pad, head), 0)
    lane = lax.broadcasted_iota(jnp.int32, (pad, head), 1)

    def prepare(which, place, pkbuf, pvbuf):
        device = 2 * chip + which
        ids, dead = [], []
        shift = jnp.zeros((pad, head), jnp.int32)
        for i in range(nb):
            e = lax.rem(device - i + n, n)
            slot = jnp.int32(0)
            for j in range(1, nb):
                slot = jnp.where(owner_ref[e, j] == device, j, slot)
            ids.append(id_ref[e, slot])
            shift = jnp.where(row == i, blk * (prefix[e] + slot) - old_ref[e, slot], shift)
            dead.append(jnp.where(slot < count_ref[e], F32(0.0), F32(-NEG)))
        angles = shift.astype(F32) * freq_ref[0:1, :]
        cosine = jnp.cos(angles)
        sine = jnp.sin(angles)
        sine = jnp.where(lane < head // 2, -sine, sine)

        def fill():
            for i in range(nb):
                at = (place * nb + i) * blk
                x = pkbuf[ids[i]].astype(F32)
                turned = x * cosine[i : i + 1] + pltpu.roll(x, head // 2, 1) * sine[i : i + 1]
                kbuf[at : at + blk, :] = turned.astype(BF16)
                vbuf[0:head, at : at + blk] = pvbuf[ids[i]].T

        return dead, fill

    slots = 2 * nb
    vbuf[head : head + 16, :] = jnp.ones((16, slots * blk), BF16)
    dead_own, fill_own = prepare(c, 0, pk_own, pv_own)
    load_k.wait()
    load_v.wait()
    fill_own()

    def got(slot):
        q_copy(slot, z_send.at[0], chip).wait_recv()

    def pass_on(k):
        got(chip_at(k, 0))
        q_copy(chip_at(k, 0), y_send.at[k], y_chip).start()

    dead_other, fill_other = prepare(1 - c, 1, pk_other, pv_other)
    for d in shared:
        d.wait_recv()
    fill_other()
    dead = dead_own + dead_other

    scale = math.log2(math.e) / math.sqrt(head)
    nt = (((1,), (1,)), ((), ()))
    new_k = jnp.concatenate([nk_ref[...].astype(F32), nkbuf[...].astype(F32)], axis=0).astype(BF16)
    new_v = jnp.concatenate([nv_ref[...].astype(F32), nvbuf[...].astype(F32)], axis=0)
    new_v = jnp.concatenate([new_v.T, jnp.ones((16, 2 * fresh), F32)], axis=0).astype(BF16)
    fresh_at = lax.broadcasted_iota(jnp.int32, (2 * fresh, rows), 0)
    fresh_at = jnp.where(
        fresh_at < fresh, me * fresh + fresh_at, other * fresh + fresh_at - fresh
    )
    token_at = lax.broadcasted_iota(jnp.int32, (2 * fresh, rows), 1) // group
    some = 4

    def attend(p, to, r, held):
        if to is not None:
            sb, tb, fb = to
            q = qbuf[p]
            fresh_s = lax.dot_general(new_k, q, nt, preferred_element_type=F32)
            visible = fresh_at <= (2 * p + c) * fresh + token_at
            fresh_s = jnp.where(visible, fresh_s, NEG)
            top = jnp.broadcast_to(jnp.max(fresh_s, axis=0, keepdims=True), (8, rows))
        if held is not None:
            hs, ht, hf = held
            was = ht[0:1, :]
        for i in range(0, slots, some):
            if to is not None:
                s = lax.dot_general(
                    kbuf[i * blk : (i + some) * blk, :], q, nt, preferred_element_type=F32
                )
                sb[i * blk : (i + some) * blk, :] = s
                for j in range(some):
                    part = s[j * blk : (j + 1) * blk].reshape(blk // 8, 8, rows)
                    top = jnp.maximum(top, jnp.max(part, axis=0) - dead[i + j])
            if held is not None:
                for j in range(i, i + some):
                    s = hs[j * blk : (j + 1) * blk, :]
                    w = jnp.exp2(s * scale - (was + dead[j]))
                    pbuf[j * blk : (j + 1) * blk, :] = w.astype(BF16)
        if held is not None:
            summed = jnp.dot(vbuf[...], pbuf[...], preferred_element_type=F32)
            summed = summed + jnp.dot(new_v, hf[...], preferred_element_type=F32)
            sums = summed[head : head + 1]
            some_live = sums > 0
            lse = jnp.where(some_live, was + jnp.log2(jnp.where(some_live, sums, 1.0)), NEG)
            outbuf[r] = pack(summed[:head] * jnp.where(some_live, 1.0 / sums, 0.0), lse)
        if to is not None:
            top = jnp.max(top, axis=0, keepdims=True) * scale
            tb[...] = jnp.broadcast_to(top, (8, rows))
            fb[...] = jnp.where(visible, jnp.exp2(fresh_s * scale - top), 0.0).astype(BF16)

    def final_copy(r, p):
        return copy(outbuf.at[r], fbuf.at[chip], f_send.at[r], f_recv.at[chip], 2 * p + c)

    own = chips - 1

    def chunk_at(r):
        k = jnp.where(lax.rem(r, nz) == nz - 1, 0, lax.rem(lax.rem(r, nz) + 1, nz - 1) + 1)
        b = jnp.where(jnp.logical_and(r >= nz - 1, r < own), 1, 0)
        return chip_at(k, b)

    one, two = (sbuf, tbuf, wbuf), (sbuf2, tbuf2, wbuf2)

    def step(r, to, held):
        p = chunk_at(r)

        @pl.when(jnp.logical_and(r >= nz - 1, r < own))
        def _():
            got(p)

        attend(p, to, r - 1, held)
        final_copy(r - 1, chunk_at(r - 1)).start()

    def two_steps(t, _):
        step(2 * t + 1, two, one)
        step(2 * t + 2, one, two)
        return 0

    for k in far_first:
        pass_on(k)
    attend(chunk_at(jnp.int32(0)), one, None, None)
    lax.fori_loop(0, chips // 2 - 1, two_steps, 0)
    step(jnp.int32(own), two, one)
    attend(None, None, own, two)

    acc, best = unpack(outbuf[own], head)
    acc_sum = jnp.ones((1, rows), F32)
    for r in range(own):
        src = chunk_at(r)
        copy(outbuf.at[0], fbuf.at[src], f_send.at[0], f_recv.at[src], other).wait_recv()
        part, lse = unpack(fbuf[src], head)
        new = jnp.maximum(best, lse)
        f_old = jnp.exp2(best - new)
        f = jnp.exp2(lse - new)
        acc = acc * f_old + part * f
        acc_sum = acc_sum * f_old + f
        best = new
    o_ref[...] = (acc / acc_sum).T.astype(BF16)

    for d in z_copies + shared:
        d.wait_send()
    for k in range(nz):
        q_copy(chip, y_send.at[k], y_chip).wait_send()
    for r in range(own):
        final_copy(r, chip).wait_send()


def local(
    queries, new_keys, new_values, pool_keys, pool_values, block_owner, block_id, old_start,
    cached_counts,
):
    n, nb = block_owner.shape
    tokens, group, head = queries.shape
    blk = pool_keys.shape[1]
    fresh = new_keys.shape[0]
    rows = tokens * group
    chips = n // 2
    vmem = pl.BlockSpec(memory_space=pltpu.VMEM)
    smem = pl.BlockSpec(memory_space=pltpu.SMEM)
    anywhere = pl.BlockSpec(memory_space=pl.ANY)
    dma = pltpu.SemaphoreType.DMA
    keys = 2 * nb * blk
    out = pl.pallas_call(
        functools.partial(kernel, (n, nb, blk, head, rows, fresh, group)),
        out_shape=jax.ShapeDtypeStruct((rows, head), BF16),
        in_specs=[anywhere, vmem, vmem, anywhere, anywhere, vmem] + [smem] * 4,
        out_specs=vmem,
        scratch_shapes=[
            pltpu.VMEM((chips, rows, head), BF16),
            pltpu.VMEM((nb, blk, head), BF16),
            pltpu.VMEM((nb, blk, head), BF16),
            pltpu.VMEM((nb, blk, head), BF16),
            pltpu.VMEM((nb, blk, head), BF16),
            pltpu.VMEM((fresh, head), BF16),
            pltpu.VMEM((fresh, head), BF16),
            pltpu.VMEM((keys, head), BF16),
            pltpu.VMEM((head + 16, keys), BF16),
            pltpu.VMEM((keys, rows), F32),
            pltpu.VMEM((keys, rows), F32),
            pltpu.VMEM((8, rows), F32),
            pltpu.VMEM((8, rows), F32),
            pltpu.VMEM((2 * fresh, rows), BF16),
            pltpu.VMEM((2 * fresh, rows), BF16),
            pltpu.VMEM((keys, rows), BF16),
            pltpu.VMEM((chips, head + 16, rows), BF16),
            pltpu.VMEM((chips, head + 16, rows), BF16),
            pltpu.SMEM((n,), jnp.int32),
            dma((3,)),
            dma((chips,)),
            dma((n // 4,)),
            dma((n // 4,)),
            dma((4,)),
            dma((4,)),
            dma((chips,)),
            dma((chips,)),
        ],
        compiler_params=pltpu.CompilerParams(collective_id=0, has_side_effects=True),
    )(
        queries.reshape(rows, head), new_keys, new_values, pool_keys, pool_values,
        jnp.asarray(frequencies(head)), block_owner, block_id, old_start, cached_counts,
    )
    return out.reshape(tokens, group, head)


def solution(mesh):
    placed = (
        P(("groups", "ctx"), None, None),
        P(("groups", "ctx"), None),
        P(("groups", "ctx"), None),
        P(("groups", "ctx"), None, None),
        P(("groups", "ctx"), None, None),
        P("groups", None),
        P("groups", None),
        P("groups", None),
        P("groups"),
    )
    return jax.shard_map(
        local,
        mesh=mesh,
        in_specs=placed,
        out_specs=P(("groups", "ctx"), None, None),
        check_vma=False,
    )
```

profile of v0, /device:TPU:0, one launch (start us, length us, event | category | flops | bytes accessed | tf_op | source)
XLA Modules:
  0.0 22.5 jit_solution(17083839209983017097)
XLA Ops:
  0.0 21.2 %shard_map.100 = bf16[128,128]{1,0:T(8,128)(2,1)} custom-call(bf16[128,128]{1,0:T(8,128)(2,1)} %bitcast.3, bf16[8,128]{1,0:T(8,128)(2,1)} %nk_ref.1, bf16[8,128]{1,0:T(8,128)(2,1)} %nv_ref.1, bf16[12,128,128]{2,1,0:T(8,128)(2,1)} %pk_ref.1, bf16[12,128,128]{2,1,0:T(8,128)(2,1)} %pv_ref.1, f32[8,128]{1,0:T(8,128)} %constant.2.clone.freq_ref, ...), custom_call_target="tpu_custom_call" | custom-call | tf_op jit(solution)/shard_map/pallas_call | solution.py:326
  21.2 1.4 %copy.12 = bf16[8,16,128]{2,1,0:T(8,128)(2,1)} copy(bf16[8,16,128]{2,1,0:T(8,128)(2,1)} %bitcast.2) | data formatting | bytes 65536
where the time goes:
time: 22.8 us; the launch traced here: 22.5 us
  Pallas kernels  21.2 us (93%)
  local copies, waits for them, and re-layouts  1.38 us (6%)
    pallas_call x1, Pallas kernels, local(): pl.pallas_call(functools.partial(kernel, (n, nb, blk, head, rows, fresh,...  21.2 us
    unnamed x1, local copies, waits for them, and re-layouts  1.38 us

commit v1 on v0

--- a/solution.py
+++ b/solution.py
@@ -25,20 +25,50 @@
     return np.tile(freq.astype(np.float32), (8, 2))
 
 
-def pack(out, lse):
-    cols = out.shape[1]
+TAIL = 8
+
+
+def pack(out_ref, r, out, lse):
+    head, cols = out.shape
     hi = lse.astype(BF16).astype(F32)
     mid = (lse - hi).astype(BF16).astype(F32)
     low = lse - hi - mid
-    row = lax.broadcasted_iota(jnp.int32, (16, cols), 0)
+    row = lax.broadcasted_iota(jnp.int32, (TAIL, cols), 0)
     tail = jnp.where(row == 0, hi, jnp.where(row == 1, mid, jnp.where(row == 2, low, 0.0)))
-    return jnp.concatenate([out.astype(BF16), tail.astype(BF16)], axis=0)
-
-
-def unpack(message, head):
-    tail = message[head : head + 16].astype(F32)
+    out_ref[r, 0:head] = out.astype(BF16)
+    out_ref[r, head : head + TAIL] = tail.astype(BF16)
+
+
+def unpack(ref, r, head):
+    tail = ref[r, head : head + TAIL].astype(F32)
     lse = tail[0:1] + tail[1:2] + tail[2:3]
-    return message[:head].astype(F32), lse
+    return ref[r, 0:head].astype(F32), lse
+
+
+def plan(nz):
+    if nz == 4:
+        return dict(
+            greet=[(2, 0), (1, 0), (0, 1), (1, 1)],
+            greet_inner=[(3, 0), (3, 1)],
+            first=[(2, 0), (3, 0), (1, 0), (0, 1), (1, 1), (3, 1)],
+            relay={(2, 0): [(1, 0), (1, 1), (0, 1)]},
+            relay_inner=[(1, 0), (1, 1)],
+            order=[(0, 0), (0, 1), (1, 0), (1, 1), (2, 0), (3, 0), (3, 1), (2, 1)],
+            relay_at={3: [(2, 0)]},
+            flush=[5],
+        )
+    far = [*range(2, nz), 1][: nz - 1]
+    line = [(k, 0) for k in far]
+    return dict(
+        greet=line + [(0, 1)],
+        greet_inner=[],
+        first=line + [(0, 1)],
+        relay={label: [(0, 1)] for label in line},
+        relay_inner=[],
+        order=[(0, 0)] + line + [(0, 1)] + [(k, 1) for k in far],
+        relay_at={1: line},
+        flush=[],
+    )
 
 
 def kernel(
@@ -49,10 +79,10 @@
     pk_ref,
     pv_ref,
     freq_ref,
-    owner_ref,
-    id_ref,
-    old_ref,
-    count_ref,
+    owner_hbm,
+    id_hbm,
+    old_hbm,
+    count_hbm,
     o_ref,
     qbuf,
     pk_own,
@@ -61,6 +91,7 @@
     pv_other,
     nkbuf,
     nvbuf,
+    fqbuf,
     kbuf,
     vbuf,
     sbuf,
@@ -72,11 +103,15 @@
     pbuf,
     outbuf,
     fbuf,
+    owner_ref,
+    id_ref,
+    old_ref,
+    count_ref,
     prefix,
     l_sem,
     q_recv,
-    z_send,
-    y_send,
+    q_send,
+    r_send,
     x_send,
     x_recv,
     f_send,
@@ -93,6 +128,8 @@
     y = lax.rem(chip, ny)
     z = chip // ny
     other = me + 1 - 2 * c
+    todo = plan(nz)
+    inner = jnp.logical_and(z > 0, z < nz - 1)
 
     def z_at(k):
         if nz & (nz - 1):
@@ -106,22 +143,41 @@
     def chip_at(k, b):
         return z_at(k) * ny + lax.rem(y + b, ny)
 
+    def maybe(only_inner, do):
+        if only_inner:
+            pl.when(inner)(do)
+        else:
+            do()
+
     barrier = pltpu.get_barrier_semaphore()
-    for r in range(1, chips):
-        pl.semaphore_signal(
-            barrier, inc=1,
-            device_id=(grp, 2 * lax.rem(chip + r, chips) + c), device_id_type=MESH,
-        )
-    pl.semaphore_signal(barrier, inc=1, device_id=(grp, other), device_id_type=MESH)
-
-    load_q = pltpu.make_async_copy(q_ref, qbuf.at[chip], l_sem.at[0])
-    load_k = pltpu.make_async_copy(pk_ref, pk_own, l_sem.at[1])
-    load_v = pltpu.make_async_copy(pv_ref, pv_own, l_sem.at[2])
-    load_q.start()
-    load_k.start()
-    load_v.start()
-    load_q.wait()
-    pl.semaphore_wait(barrier, chips)
+
+    def greet(to):
+        pl.semaphore_signal(barrier, inc=1, device_id=(grp, to), device_id_type=MESH)
+
+    for label in todo["greet"]:
+        greet(2 * chip_at(*label) + c)
+    for label in todo["greet_inner"]:
+        maybe(True, lambda label=label: greet(2 * chip_at(*label) + c))
+    greet(other)
+
+    def load(i, src, dst):
+        return pltpu.make_async_copy(src, dst, l_sem.at[i])
+
+    load_small = [
+        load(0, owner_hbm, owner_ref),
+        load(1, id_hbm, id_ref),
+        load(2, old_hbm, old_ref),
+        load(3, count_hbm, count_ref),
+        load(4, freq_ref, fqbuf),
+    ]
+    load_new = [
+        load(5, q_ref, qbuf.at[chip]),
+        load(6, nk_ref, nkbuf.at[0]),
+        load(7, nv_ref, nvbuf.at[0]),
+    ]
+    load_pool = [load(8, pk_ref, pk_own), load(9, pv_ref, pv_own)]
+    for d in load_small + load_new + load_pool:
+        d.start()
 
     def copy(src, dst, ss, rs, to):
         return pltpu.make_async_remote_copy(
@@ -132,20 +188,8 @@
     def q_copy(slot, ss, to_chip):
         return copy(qbuf.at[slot], qbuf.at[slot], ss, q_recv.at[slot], 2 * to_chip + c)
 
-    y_chip = chip_at(0, 1)
-    far_first = [*range(2, nz), 1][: nz - 1]
-    z_copies = [q_copy(chip, z_send.at[k], chip_at(k, 0)) for k in far_first]
-    for d in z_copies:
-        d.start()
-    q_copy(chip, y_send.at[0], y_chip).start()
-    shared = [
-        copy(nk_ref, nkbuf, x_send.at[0], x_recv.at[0], other),
-        copy(nv_ref, nvbuf, x_send.at[1], x_recv.at[1], other),
-        copy(pk_ref, pk_other, x_send.at[2], x_recv.at[2], other),
-        copy(pv_ref, pv_other, x_send.at[3], x_recv.at[3], other),
-    ]
-    for d in shared:
-        d.start()
+    for d in load_small:
+        d.wait()
 
     total = jnp.int32(0)
     for e in range(n):
@@ -168,7 +212,7 @@
             ids.append(id_ref[e, slot])
             shift = jnp.where(row == i, blk * (prefix[e] + slot) - old_ref[e, slot], shift)
             dead.append(jnp.where(slot < count_ref[e], F32(0.0), F32(-NEG)))
-        angles = shift.astype(F32) * freq_ref[0:1, :]
+        angles = shift.astype(F32) * fqbuf[0:1, :]
         cosine = jnp.cos(angles)
         sine = jnp.sin(angles)
         sine = jnp.where(lane < head // 2, -sine, sine)
@@ -186,27 +230,50 @@
     slots = 2 * nb
     vbuf[head : head + 16, :] = jnp.ones((16, slots * blk), BF16)
     dead_own, fill_own = prepare(c, 0, pk_own, pv_own)
-    load_k.wait()
-    load_v.wait()
+    dead_other, fill_other = prepare(1 - c, 1, pk_other, pv_other)
+    dead = dead_own + dead_other
+    for d in load_new + load_pool:
+        d.wait()
     fill_own()
 
+    maybe_inner = todo["greet_inner"]
+    pl.semaphore_wait(barrier, len(todo["greet"]) + 1 + jnp.where(inner, len(maybe_inner), 0))
+
+    def send_own(label):
+        return q_copy(chip, q_send.at[todo["first"].index(label)], chip_at(*label))
+
+    for label in todo["first"]:
+        maybe(label in maybe_inner, lambda label=label: send_own(label).start())
+    shared = [
+        copy(pk_own, pk_other, x_send.at[2], x_recv.at[2], other),
+        copy(pv_own, pv_other, x_send.at[3], x_recv.at[3], other),
+        copy(nkbuf.at[0], nkbuf.at[1], x_send.at[0], x_recv.at[0], other),
+        copy(nvbuf.at[0], nvbuf.at[1], x_send.at[1], x_recv.at[1], other),
+    ]
+    for d in shared:
+        d.start()
+
     def got(slot):
-        q_copy(slot, z_send.at[0], chip).wait_recv()
-
-    def pass_on(k):
-        got(chip_at(k, 0))
-        q_copy(chip_at(k, 0), y_send.at[k], y_chip).start()
-
-    dead_other, fill_other = prepare(1 - c, 1, pk_other, pv_other)
+        q_copy(slot, q_send.at[0], chip).wait_recv()
+
+    relays = [(src, to) for src in todo["relay"] for to in todo["relay"][src]]
+
+    def relay_copy(src, to):
+        return q_copy(chip_at(*src), r_send.at[relays.index((src, to))], chip_at(*to))
+
+    def pass_on(src):
+        got(chip_at(*src))
+        for to in todo["relay"][src]:
+            maybe(to in todo["relay_inner"], lambda to=to: relay_copy(src, to).start())
+
     for d in shared:
         d.wait_recv()
     fill_other()
-    dead = dead_own + dead_other
 
     scale = math.log2(math.e) / math.sqrt(head)
     nt = (((1,), (1,)), ((), ()))
-    new_k = jnp.concatenate([nk_ref[...].astype(F32), nkbuf[...].astype(F32)], axis=0).astype(BF16)
-    new_v = jnp.concatenate([nv_ref[...].astype(F32), nvbuf[...].astype(F32)], axis=0)
+    new_k = jnp.concatenate([nkbuf[0].astype(F32), nkbuf[1].astype(F32)], axis=0).astype(BF16)
+    new_v = jnp.concatenate([nvbuf[0].astype(F32), nvbuf[1].astype(F32)], axis=0)
     new_v = jnp.concatenate([new_v.T, jnp.ones((16, 2 * fresh), F32)], axis=0).astype(BF16)
     fresh_at = lax.broadcasted_iota(jnp.int32, (2 * fresh, rows), 0)
     fresh_at = jnp.where(
@@ -246,7 +313,7 @@
             sums = summed[head : head + 1]
             some_live = sums > 0
             lse = jnp.where(some_live, was + jnp.log2(jnp.where(some_live, sums, 1.0)), NEG)
-            outbuf[r] = pack(summed[:head] * jnp.where(some_live, 1.0 / sums, 0.0), lse)
+            pack(outbuf, r, summed[:head] * jnp.where(some_live, 1.0 / sums, 0.0), lse)
         if to is not None:
             top = jnp.max(top, axis=0, keepdims=True) * scale
             tb[...] = jnp.broadcast_to(top, (8, rows))
@@ -255,43 +322,80 @@
     def final_copy(r, p):
         return copy(outbuf.at[r], fbuf.at[chip], f_send.at[r], f_recv.at[chip], 2 * p + c)
 
-    own = chips - 1
+    order = todo["order"]
+    relayed = [order.index(src) for src in todo["relay"]]
 
     def chunk_at(r):
-        k = jnp.where(lax.rem(r, nz) == nz - 1, 0, lax.rem(lax.rem(r, nz) + 1, nz - 1) + 1)
-        b = jnp.where(jnp.logical_and(r >= nz - 1, r < own), 1, 0)
+        if isinstance(r, int):
+            return chip_at(*order[r])
+        k, b = jnp.int32(0), jnp.int32(0)
+        for i, (ki, bi) in enumerate(order):
+            k = jnp.where(r == i, ki, k)
+            b = jnp.where(r == i, bi, b)
         return chip_at(k, b)
 
-    one, two = (sbuf, tbuf, wbuf), (sbuf2, tbuf2, wbuf2)
-
-    def step(r, to, held):
-        p = chunk_at(r)
-
-        @pl.when(jnp.logical_and(r >= nz - 1, r < own))
-        def _():
-            got(p)
-
-        attend(p, to, r - 1, held)
-        final_copy(r - 1, chunk_at(r - 1)).start()
-
-    def two_steps(t, _):
-        step(2 * t + 1, two, one)
-        step(2 * t + 2, one, two)
-        return 0
-
-    for k in far_first:
-        pass_on(k)
-    attend(chunk_at(jnp.int32(0)), one, None, None)
-    lax.fori_loop(0, chips // 2 - 1, two_steps, 0)
-    step(jnp.int32(own), two, one)
-    attend(None, None, own, two)
-
-    acc, best = unpack(outbuf[own], head)
+    buffers = [(sbuf, tbuf, wbuf), (sbuf2, tbuf2, wbuf2)]
+
+    def ready(r, p):
+        if isinstance(r, int):
+            if r not in relayed:
+                got(p)
+        else:
+            @pl.when(r >= 1 + len(relayed))
+            def _():
+                got(p)
+
+    def out(r):
+        final_copy(r, chunk_at(r)).start()
+
+    attend(chip, buffers[0], None, None)
+    if chips <= 8:
+        held = 0
+        for r in range(1, chips):
+            for src in todo["relay_at"].get(r, []):
+                pass_on(src)
+            if r in todo["flush"]:
+                attend(None, None, held, buffers[held % 2])
+                if held:
+                    out(held)
+                held = None
+            p = chunk_at(r)
+            ready(r, p)
+            attend(p, buffers[r % 2], held, None if held is None else buffers[held % 2])
+            if held:
+                out(held)
+            held = r
+        attend(None, None, held, buffers[held % 2])
+        out(held)
+    else:
+        for src in todo["relay_at"][1]:
+            pass_on(src)
+
+        def step(r, to, held):
+            p = chunk_at(r)
+            ready(r, p)
+            attend(p, to, r - 1, held)
+
+            @pl.when(r > 1)
+            def _():
+                out(r - 1)
+
+        def two_steps(t, _):
+            step(2 * t + 1, buffers[1], buffers[0])
+            step(2 * t + 2, buffers[0], buffers[1])
+            return 0
+
+        lax.fori_loop(0, chips // 2 - 1, two_steps, 0)
+        step(jnp.int32(chips - 1), buffers[1], buffers[0])
+        attend(None, None, chips - 1, buffers[1])
+        out(jnp.int32(chips - 1))
+
+    acc, best = unpack(outbuf, 0, head)
     acc_sum = jnp.ones((1, rows), F32)
-    for r in range(own):
+    for r in range(1, chips):
         src = chunk_at(r)
         copy(outbuf.at[0], fbuf.at[src], f_send.at[0], f_recv.at[src], other).wait_recv()
-        part, lse = unpack(fbuf[src], head)
+        part, lse = unpack(fbuf, src, head)
         new = jnp.maximum(best, lse)
         f_old = jnp.exp2(best - new)
         f = jnp.exp2(lse - new)
@@ -300,11 +404,13 @@
         best = new
     o_ref[...] = (acc / acc_sum).T.astype(BF16)
 
-    for d in z_copies + shared:
+    for d in shared:
         d.wait_send()
-    for k in range(nz):
-        q_copy(chip, y_send.at[k], y_chip).wait_send()
-    for r in range(own):
+    for label in todo["first"]:
+        maybe(label in maybe_inner, lambda label=label: send_own(label).wait_send())
+    for src, to in relays:
+        maybe(to in todo["relay_inner"], lambda src=src, to=to: relay_copy(src, to).wait_send())
+    for r in range(1, chips):
         final_copy(r, chip).wait_send()
 
 
@@ -318,15 +424,15 @@
     fresh = new_keys.shape[0]
     rows = tokens * group
     chips = n // 2
+    todo = plan(n // 4)
     vmem = pl.BlockSpec(memory_space=pltpu.VMEM)
-    smem = pl.BlockSpec(memory_space=pltpu.SMEM)
-    anywhere = pl.BlockSpec(memory_space=pl.ANY)
+    hbm = pl.BlockSpec(memory_space=pltpu.HBM)
     dma = pltpu.SemaphoreType.DMA
     keys = 2 * nb * blk
     out = pl.pallas_call(
         functools.partial(kernel, (n, nb, blk, head, rows, fresh, group)),
         out_shape=jax.ShapeDtypeStruct((rows, head), BF16),
-        in_specs=[anywhere, vmem, vmem, anywhere, anywhere, vmem] + [smem] * 4,
+        in_specs=[hbm] * 10,
         out_specs=vmem,
         scratch_shapes=[
             pltpu.VMEM((chips, rows, head), BF16),
@@ -334,8 +440,9 @@
             pltpu.VMEM((nb, blk, head), BF16),
             pltpu.VMEM((nb, blk, head), BF16),
             pltpu.VMEM((nb, blk, head), BF16),
-            pltpu.VMEM((fresh, head), BF16),
-            pltpu.VMEM((fresh, head), BF16),
+            pltpu.VMEM((2, fresh, head), BF16),
+            pltpu.VMEM((2, fresh, head), BF16),
+            pltpu.VMEM((8, head), F32),
             pltpu.VMEM((keys, head), BF16),
             pltpu.VMEM((head + 16, keys), BF16),
             pltpu.VMEM((keys, rows), F32),
@@ -345,23 +452,29 @@
             pltpu.VMEM((2 * fresh, rows), BF16),
             pltpu.VMEM((2 * fresh, rows), BF16),
             pltpu.VMEM((keys, rows), BF16),
-            pltpu.VMEM((chips, head + 16, rows), BF16),
-            pltpu.VMEM((chips, head + 16, rows), BF16),
+            pltpu.VMEM((chips, head + TAIL, rows), BF16),
+            pltpu.VMEM((chips, head + TAIL, rows), BF16),
+            pltpu.SMEM(block_owner.shape, jnp.int32),
+            pltpu.SMEM(block_id.shape, jnp.int32),
+            pltpu.SMEM(old_start.shape, jnp.int32),
+            pltpu.SMEM(cached_counts.shape, jnp.int32),
             pltpu.SMEM((n,), jnp.int32),
-            dma((3,)),
+            dma((10,)),
             dma((chips,)),
-            dma((n // 4,)),
-            dma((n // 4,)),
+            dma((len(todo["first"]),)),
+            dma((sum(len(v) for v in todo["relay"].values()),)),
             dma((4,)),
             dma((4,)),
             dma((chips,)),
             dma((chips,)),
         ],
-        compiler_params=pltpu.CompilerParams(collective_id=0, has_side_effects=True),
-    )(
+        compiler_params=pltpu.CompilerParams(
+            collective_id=0, has_side_effects=True, vmem_limit_bytes=48 * 1024 * 1024
+        ),
+    )(*[pltpu.with_memory_space_constraint(v, pltpu.HBM) for v in (
         queries.reshape(rows, head), new_keys, new_values, pool_keys, pool_values,
         jnp.asarray(frequencies(head)), block_owner, block_id, old_start, cached_counts,
-    )
+    )])
     return out.reshape(tokens, group, head)
 
 

time: 22.8 us -> 22.3 us (0.978)
  local copies, waits for them, and re-layouts: 1.38 us -> 0.62 us
    unnamed x1, local copies, waits for them, and re-layouts: 1.38 us -> 0.62 us
    pallas_call x1, Pallas kernels: 21.2 us -> 21.4 us  [local(): pl.pallas_call(functools.partial(kernel, (n, nb, blk, head, rows, fresh,...]
where the time goes in v1:
time: 22.3 us; the launch traced here: 22.1 us
  Pallas kernels  21.4 us (96%)
  local copies, waits for them, and re-layouts  0.62 us (3%)
    pallas_call x1, Pallas kernels, local(): pl.pallas_call(functools.partial(kernel, (n, nb, blk, head, rows, fresh,...  21.4 us
    unnamed x1, local copies, waits for them, and re-layouts  0.62 us

profile of v1, /device:TPU:0, one launch (start us, length us, event | category | flops | bytes accessed | tf_op | source)
XLA Modules:
  0.0 22.1 jit_solution(7142419928713825806)
XLA Ops:
  0.0 21.4 %shard_map.100 = bf16[128,128]{1,0:T(8,128)(2,1)S(1)} custom-call(bf16[128,128]{1,0:T(8,128)(2,1)} %bitcast.3, bf16[8,128]{1,0:T(8,128)(2,1)} %nk_ref.1, bf16[8,128]{1,0:T(8,128)(2,1)} %nv_ref.1, bf16[12,128,128]{2,1,0:T(8,128)(2,1)} %pk_ref.1, bf16[12,128,128]{2,1,0:T(8,128)(2,1)} %pv_ref.1, f32[8,128]{1,0:T(8,128)} %constant.2.clone.freq_ref, ...), custom_call_target="tpu_custom_call" | custom-call | tf_op jit(solution)/shard_map/pallas_call | solution.py:432
  21.4 0.6 %copy.12 = bf16[8,16,128]{2,1,0:T(8,128)(2,1)} copy(bf16[8,16,128]{2,1,0:T(8,128)(2,1)S(1)} %bitcast.2) | data formatting | bytes 65536

commit v2 on v1

--- a/solution.py
+++ b/solution.py
@@ -53,9 +53,11 @@
             first=[(2, 0), (3, 0), (1, 0), (0, 1), (1, 1), (3, 1)],
             relay={(2, 0): [(1, 0), (1, 1), (0, 1)]},
             relay_inner=[(1, 0), (1, 1)],
-            order=[(0, 0), (0, 1), (1, 0), (1, 1), (2, 0), (3, 0), (3, 1), (2, 1)],
+            order=[(0, 0), (0, 1), (1, 0), (1, 1), (2, 0), (3, 1), (3, 0), (2, 1)],
             relay_at={3: [(2, 0)]},
             flush=[5],
+            keep=[1, 2, 3],
+            let_go=6,
         )
     far = [*range(2, nz), 1][: nz - 1]
     line = [(k, 0) for k in far]
@@ -230,11 +232,7 @@
     slots = 2 * nb
     vbuf[head : head + 16, :] = jnp.ones((16, slots * blk), BF16)
     dead_own, fill_own = prepare(c, 0, pk_own, pv_own)
-    dead_other, fill_other = prepare(1 - c, 1, pk_other, pv_other)
-    dead = dead_own + dead_other
-    for d in load_new + load_pool:
-        d.wait()
-    fill_own()
+    load_new[0].wait()
 
     maybe_inner = todo["greet_inner"]
     pl.semaphore_wait(barrier, len(todo["greet"]) + 1 + jnp.where(inner, len(maybe_inner), 0))
@@ -250,8 +248,13 @@
         copy(nkbuf.at[0], nkbuf.at[1], x_send.at[0], x_recv.at[0], other),
         copy(nvbuf.at[0], nvbuf.at[1], x_send.at[1], x_recv.at[1], other),
     ]
+    for d in load_new[1:] + load_pool:
+        d.wait()
     for d in shared:
         d.start()
+    fill_own()
+    dead_other, fill_other = prepare(1 - c, 1, pk_other, pv_other)
+    dead = dead_own + dead_other
 
     def got(slot):
         q_copy(slot, q_send.at[0], chip).wait_recv()
@@ -351,6 +354,7 @@
     attend(chip, buffers[0], None, None)
     if chips <= 8:
         held = 0
+        kept = []
         for r in range(1, chips):
             for src in todo["relay_at"].get(r, []):
                 pass_on(src)
@@ -362,8 +366,14 @@
             p = chunk_at(r)
             ready(r, p)
             attend(p, buffers[r % 2], held, None if held is None else buffers[held % 2])
-            if held:
+            if held in todo["keep"]:
+                kept.append(held)
+            elif held:
                 out(held)
+            if r == todo["let_go"]:
+                for h in kept:
+                    out(h)
+                kept = []
             held = r
         attend(None, None, held, buffers[held % 2])
         out(held)

time: 22.3 us -> 21.1 us (0.946)
  Pallas kernels: 21.4 us -> 20.3 us
    pallas_call x1, Pallas kernels: 21.4 us -> 20.3 us  [local(): pl.pallas_call(functools.partial(kernel, (n, nb, blk, head, rows, fresh,...]
where the time goes in v2:
time: 21.1 us; the launch traced here: 20.9 us
  Pallas kernels  20.3 us (96%)
  local copies, waits for them, and re-layouts  0.62 us (3%)
    pallas_call x1, Pallas kernels, local(): pl.pallas_call(functools.partial(kernel, (n, nb, blk, head, rows, fresh,...  20.3 us
    unnamed x1, local copies, waits for them, and re-layouts  0.62 us

profile of v2, /device:TPU:0, one launch (start us, length us, event | category | flops | bytes accessed | tf_op | source)
XLA Modules:
  0.0 20.9 jit_solution(11283950448301134177)
XLA Ops:
  0.0 20.3 %shard_map.100 = bf16[128,128]{1,0:T(8,128)(2,1)S(1)} custom-call(bf16[128,128]{1,0:T(8,128)(2,1)} %bitcast.3, bf16[8,128]{1,0:T(8,128)(2,1)} %nk_ref.1, bf16[8,128]{1,0:T(8,128)(2,1)} %nv_ref.1, bf16[12,128,128]{2,1,0:T(8,128)(2,1)} %pk_ref.1, bf16[12,128,128]{2,1,0:T(8,128)(2,1)} %pv_ref.1, f32[8,128]{1,0:T(8,128)} %constant.2.clone.freq_ref, ...), custom_call_target="tpu_custom_call" | custom-call | tf_op jit(solution)/shard_map/pallas_call | solution.py:442
  20.3 0.6 %copy.12 = bf16[8,16,128]{2,1,0:T(8,128)(2,1)} copy(bf16[8,16,128]{2,1,0:T(8,128)(2,1)S(1)} %bitcast.2) | data formatting | bytes 65536

commit v3 on v2

--- a/solution.py
+++ b/solution.py
@@ -58,6 +58,7 @@
             flush=[5],
             keep=[1, 2, 3],
             let_go=6,
+            by_y=[5, 6],
         )
     far = [*range(2, nz), 1][: nz - 1]
     line = [(k, 0) for k in far]
@@ -70,6 +71,7 @@
         order=[(0, 0)] + line + [(0, 1)] + [(k, 1) for k in far],
         relay_at={1: line},
         flush=[],
+        by_y=[],
     )
 
 
@@ -329,6 +331,8 @@
     relayed = [order.index(src) for src in todo["relay"]]
 
     def chunk_at(r):
+        if isinstance(r, int) and r in todo["by_y"]:
+            return z_at(order[r][0]) * ny + todo["by_y"].index(r)
         if isinstance(r, int):
             return chip_at(*order[r])
         k, b = jnp.int32(0), jnp.int32(0)

time: 21.1 us -> 20.3 us (0.962)
  Pallas kernels: 20.3 us -> 19.5 us
    pallas_call x1, Pallas kernels: 20.3 us -> 19.5 us  [local(): pl.pallas_call(functools.partial(kernel, (n, nb, blk, head, rows, fresh,...]
where the time goes in v3:
time: 20.3 us; the launch traced here: 20.1 us
  Pallas kernels  19.5 us (96%)
  local copies, waits for them, and re-layouts  0.62 us (3%)
    pallas_call x1, Pallas kernels, local(): pl.pallas_call(functools.partial(kernel, (n, nb, blk, head, rows, fresh,...  19.5 us
    unnamed x1, local copies, waits for them, and re-layouts  0.62 us

profile of v3, /device:TPU:0, one launch (start us, length us, event | category | flops | bytes accessed | tf_op | source)
XLA Modules:
  0.0 20.1 jit_solution(3659546792162520136)
XLA Ops:
  0.0 19.5 %shard_map.100 = bf16[128,128]{1,0:T(8,128)(2,1)S(1)} custom-call(bf16[128,128]{1,0:T(8,128)(2,1)} %bitcast.3, bf16[8,128]{1,0:T(8,128)(2,1)} %nk_ref.1, bf16[8,128]{1,0:T(8,128)(2,1)} %nv_ref.1, bf16[12,128,128]{2,1,0:T(8,128)(2,1)} %pk_ref.1, bf16[12,128,128]{2,1,0:T(8,128)(2,1)} %pv_ref.1, f32[8,128]{1,0:T(8,128)} %constant.2.clone.freq_ref, ...), custom_call_target="tpu_custom_call" | custom-call | tf_op jit(solution)/shard_map/pallas_call | solution.py:446
  19.5 0.6 %copy.12 = bf16[8,16,128]{2,1,0:T(8,128)(2,1)} copy(bf16[8,16,128]{2,1,0:T(8,128)(2,1)S(1)} %bitcast.2) | data formatting | bytes 65536
